TPU v7x, 32 devices: a whole 2x2x4 slice. The times are simulated.
32 devices in a mesh: member: 2 (over x), slab: 16 (over z, y, core).
Axes of the slice: x: 2, y: 2, z: 4, core: 2. Of those that a mesh axis runs over, the one named last changes fastest.
Arguments:
- prior_ensemble_fields: float32 [64, 6, 128, 1, 1024], P('member', None, 'slab'), may hold values from -6 to 6
- params: float32 [64, 12], P('member'), may hold values from -3 to 3
- influence: int32 [12, 6], replicated, may hold values 0 or 1
- obs_cell: int32 [128, 2, 128], P('slab', 'member'), may hold values from 0 to 3071
- obs_value: float32 [128, 2, 128], P('slab', 'member'), may hold values from -6 to 6
- obs_prec: float32 [128, 2, 128], P('slab', 'member'), may hold values from 0.5 to 4
- cutoff: int32 [128], P('slab'), may hold values from 4 to 8, as said below
Outputs:
- analysis: bfloat16 [64, 6, 128, 1, 1024], P('member', None, 'slab')
- param_analysis: float32 [64, 12], P('member')
Inputs may be any that keep to these rules, and one draw needn't show every extreme that they name: `obs_cell`: index = field * 512 + level * 512 + column within the block. `cutoff`: 8 is reached by some rows.
All inputs are finite; a program needn't handle non-finite values.
Results may differ from a plain program's by a relative error of at most 0.0056.
Values may be sent and summed in bfloat16 or wider, within the bound.
No kernel may reach another device: no remote copies, remote signals or barrier semaphores. Data moves between devices by JAX's collectives and lax.ppermute only.
A program may use at most 128 MiB of HBM per device.

v0:
```python
import math
import jax
import jax.numpy as jnp
from jax import lax
from jax.sharding import PartitionSpec as P

HALO = 8
STEPS = 4
NS_STEPS = 5
diffusion = 0.2
advection = 0.15
vertical = 0.1
coupling = 0.2


def with_halo(block, sides, width):
    for axis, dim in sides:
        count = lax.axis_size(axis)
        forward = [(i, i + 1) for i in range(count - 1)]
        backward = [(target, source) for source, target in forward]
        low = lax.ppermute(
            lax.slice_in_dim(block, block.shape[dim] - width, None, axis=dim), axis, forward
        )
        high = lax.ppermute(lax.slice_in_dim(block, 0, width, axis=dim), axis, backward)
        block = jnp.concatenate([low, block, high], axis=dim)
    return block


def advance(current, dynamics_parameter):
    middle = current[:, :, 1:-1]
    upper = current[:, :, 2:]
    lower = current[:, :, :-2]
    right_col = jnp.roll(middle, -1, 4)
    left_col = jnp.roll(middle, 1, 4)
    laplace = upper + lower + right_col + left_col - 4.0 * middle
    return (
        middle
        + diffusion * laplace
        - advection * (right_col - left_col)
        + vertical * (jnp.roll(middle, 1, 3) - middle)
        + coupling * dynamics_parameter[:, :, None, None, None] * jnp.roll(middle, -1, 1)
    )


def body(prior_ensemble_fields, params, influence, obs_cell, obs_value, obs_prec, cutoff):
    highest = lax.Precision.HIGHEST
    members_here = prior_ensemble_fields.shape[0]
    rows = prior_ensemble_fields.shape[2]
    dynamics_parameter = jnp.dot(params, influence.astype(jnp.float32), precision=highest)
    prognostic_vector = prior_ensemble_fields
    for step_idx in range(STEPS):
        padded = with_halo(prognostic_vector, (("slab", 2),), 1)
        prognostic_vector = advance(padded, dynamics_parameter)
    propagate_timestep = prognostic_vector.astype(jnp.bfloat16)
    latitude_band = lax.all_to_all(
        propagate_timestep, "member", split_axis=4, concat_axis=0, tiled=True
    )
    xfull = latitude_band.astype(jnp.float32)
    ensemble = xfull.shape[0]
    block_cols = xfull.shape[4]
    levels_here = xfull.shape[3]
    xbar = jnp.mean(xfull, axis=0)
    xpert = xfull - xbar
    cells = obs_cell[:, 0, :]
    values = obs_value[:, 0, :]
    precs = obs_prec[:, 0, :]
    kinds = cells // (levels_here * block_cols)
    levels = cells // block_cols % levels_here
    columns = cells % block_cols
    row_index = jnp.arange(rows, dtype=jnp.int32)[:, None]
    ens_obs = xfull[:, kinds, row_index, levels, columns]
    ybar = jnp.mean(ens_obs, axis=0)
    ypert = ens_obs - ybar
    weighted = precs * (values - ybar)
    radius = cutoff.astype(jnp.float32)
    gram = jnp.einsum("ero,fro->ref", ypert * precs[None], ypert, precision=highest)
    gvec = jnp.einsum("ero,ro->re", ypert, weighted, precision=highest)
    stacked = jnp.concatenate([gram, gvec[:, None, :]], 1)
    wide = with_halo(stacked, (("slab", 0),), HALO)
    local = jnp.zeros_like(stacked)
    for offset in range(-HALO, HALO + 1):
        weight = jnp.maximum(0.0, 1.0 - abs(offset) / (radius + 1.0))
        local = local + weight[:, None, None] * wide[HALO + offset : HALO + offset + rows]
    gram_loc = local[:, :ensemble]
    gvec_loc = local[:, ensemble]
    eye_mat = jnp.eye(ensemble, dtype=jnp.float32)
    amat = (ensemble - 1.0) * eye_mat + gram_loc
    scale = jnp.sqrt(jnp.sum(amat * amat, axis=(1, 2)))
    ymat = amat / scale[:, None, None]
    zmat = jnp.broadcast_to(eye_mat, amat.shape)
    for step_idx in range(NS_STEPS):
        middle = 1.5 * eye_mat - 0.5 * jnp.matmul(zmat, ymat, precision=highest)
        ymat = jnp.matmul(ymat, middle, precision=highest)
        zmat = jnp.matmul(middle, zmat, precision=highest)
    wpert = math.sqrt(ensemble - 1.0) * zmat / jnp.sqrt(scale)[:, None, None]
    inner = jnp.matmul(zmat, gvec_loc[:, :, None], precision=highest)
    wbar = jnp.matmul(zmat, inner, precision=highest)[:, :, 0] / scale[:, None]
    weights = wpert + wbar[:, :, None]
    update = jnp.einsum("jfrlc,rje->efrlc", xpert, weights, precision=highest)
    analysed = (xbar + update).astype(jnp.bfloat16)
    analysis = lax.all_to_all(analysed, "member", split_axis=0, concat_axis=4, tiled=True)
    every_param = lax.all_gather(params, "member", axis=0, tiled=True)
    pbar = jnp.mean(every_param, axis=0)
    ppert = every_param - pbar
    weight_rows = jnp.sum(weights, axis=0)
    regions = rows * lax.axis_size("slab") * lax.axis_size("member")
    start = lax.axis_index("member") * members_here
    summed = lax.psum(weight_rows, ("member", "slab")) / regions
    own_cols = lax.dynamic_slice_in_dim(summed, start, members_here, 1)
    param_analysis = pbar + jnp.einsum("jk,je->ek", ppert, own_cols, precision=highest)
    return (analysis, param_analysis)


def solution(mesh):
    in_specs = (
        P("member", None, "slab", None, None),
        P("member", None),
        P(),
        P("slab", "member", None),
        P("slab", "member", None),
        P("slab", "member", None),
        P("slab"),
    )
    out_specs = (P("member", None, "slab", None, None), P("member", None))
    return jax.shard_map(body, mesh=mesh, in_specs=in_specs, out_specs=out_specs, check_vma=False)
```

profile of v0, /device:TPU:0, one launch (start us, length us, event | category | flops | bytes accessed | tf_op | source)
XLA Modules:
  0.0 462.1 jit_solution(5289665524190053646)
XLA Ops:
  0.6 6.5 %copy.281 = f32[32,6,8,1,1024]{4,0,3,2,1:T(8,128)S(1)} copy(f32[32,6,8,1,1024]{4,3,2,1,0:T(1,128)} %param.7) | data formatting | bytes 12582912 | tf_op args[0]
  7.2 2.7 copy-done.3
  9.9 1.2 fusion.110
  11.1 1.3 collective-permute-start
  12.4 4.0 collective-permute-start.1
  16.4 18.8 %fusion.108 = (f32[32,6,8,1,1023]{4,3,2,1,0:T(1,128)}, f32[32,6,8,1,1023]{4,3,2,1,0:T(1,128)}) fusion(f32[32,6,8,1,1024]{4,3,2,1,0:T(1,128)S(1)} %copy-done.2), kind=kLoop, calls=%fused_computation.186 | loop fusion | bytes 25141248 | tf_op jit(solution)/shard_map/jit(_roll_static)/slice | solution.py:33
  35.2 13.1 %slice.204 = f32[32,5,8,1,1024]{4,3,2,1,0:T(1,128)} slice(f32[32,6,8,1,1024]{4,3,2,1,0:T(1,128)} %param.7), slice={[0:32], [1:6], [0:8], [0:1], [0:1024]} | slice | bytes 10485760 | tf_op jit(solution)/shard_map/jit(_roll_static)/slice | solution.py:41
  48.4 3.9 copy.324
  52.6 1.1 pad_maximum_fusion.10
  54.2 1.6 copy.320
  56.3 4.2 copy.323
  60.5 2.4 fusion.109
  62.9 6.6 %pad_maximum_fusion.8 = (f32[32,6,8,1,1024]{4,2,3,1,0:T(8,128)S(1)}, f32[32,6,8,1,1024]{4,2,3,1,0:T(8,128)}) fusion(f32[32,6,8,1,1]{4,2,3,1,0:T(8,128)S(1)} %bitcast.105, f32[32,6,8,1,1023]{4,2,3,1,0:T(8,128)S(1)} %copy.320, f32[32,6,8,1,1023]{4,2,3,1,0:T(8,128)} %copy.323, f32[32,6,8,1,1]{4,2,3,1,0:T(8,128)S(1)} %bitcast.106), kind=kLoop, calls=%fused_computation.46 | loop fusion | flops 3145728 | bytes 25165824 | tf_op jit(solution)/shard_map/jit(_roll_static)/concatenate | solution.py:33
  69.5 20.5 %fusion.36 = f32[32,6,8,1,1024]{4,0,3,2,1:T(8,128)S(1)} fusion(f32[32,6,8,1,1024]{4,0,3,2,1:T(8,128)S(1)} %bitcast.97, f32[32,6,1,1,1024]{4,0,3,2,1:T(8,128)} %collective-permute-done.1, f32[32,6,1,1,1024]{4,0,3,2,1:T(8,128)} %collective-permute-done, f32[32,6,8,1,1024]{4,2,3,1,0:T(8,128)S(1)} %pad_maximum_fusion.10, ...), kind=kLoop, calls=%fused_computation.44 | loop fusion | flops 26738688 | bytes 33030912 | tf_op jit(solution)/shard_map/add | solution.py:37
  90.0 1.4 fusion.107
  91.4 1.3 collective-permute-start.2
  92.7 5.2 %collective-permute-start.3 = (f32[32,6,1,1,1024]{4,0,3,2,1:T(8,128)}, f32[32,6,1,1,1024]{4,0,3,2,1:T(8,128)}, u32[]{:S(2)}, u32[]{:S(2)}) collective-permute-start(f32[32,6,1,1,1024]{4,0,3,2,1:T(8,128)} %get-tuple-element.19), channel_id=1, source_target_pairs={{0,1},{1,2},{2,3},{3,4},{4,5},{5,6},{6,7},{7,8},{8,9},{9,10},{10,1... | collective-permute-start | bytes 2359304 | tf_op jit(solution)/shard_map/ppermute | solution.py:21
  97.9 1.4 fusion.106
  99.4 2.7 slice.264
  102.1 1.0 slice.265
  103.1 6.7 %fusion.105 = (f32[32,6,8,1,1023]{4,0,3,2,1:T(8,128)}, f32[32,6,8,1,1023]{4,0,3,2,1:T(8,128)}) fusion(f32[32,6,8,1,1024]{4,0,3,2,1:T(8,128)S(1)} %fusion.36), kind=kLoop, calls=%fused_computation.183 | loop fusion | bytes 25141248 | tf_op jit(solution)/shard_map/jit(_roll_static)/slice | solution.py:33
  109.9 14.1 %fusion.27 = f32[32,6,8,1,1024]{4,0,3,2,1:T(8,128)S(1)} fusion(f32[32,6,8,1,1024]{4,0,3,2,1:T(8,128)} %copy-done, f32[32,6,1,1,1024]{4,0,3,2,1:T(8,128)} %collective-permute-done.3, f32[32,6,1,1,1024]{4,0,3,2,1:T(8,128)} %collective-permute-done.2, f32[32,1,8,1,1024]{4,0,3,2,1:T(8,128)} %slice.265, f32[32,5,8,1,1024]{4,0,3,2,1:T(8,128)} %slice.264, ...), kind=kLoop, calls=%fused_computation.33 | loop fusion | flops 31457280 | bytes 33030912 | tf_op jit(solution)/shard_map/add | solution.py:37
  123.9 1.3 fusion.104
  125.2 1.3 collective-permute-start.4
  126.5 10.0 %collective-permute-start.5 = (f32[32,6,1,1,1024]{4,0,3,2,1:T(8,128)}, f32[32,6,1,1,1024]{4,0,3,2,1:T(8,128)}, u32[]{:S(2)}, u32[]{:S(2)}) collective-permute-start(f32[32,6,1,1,1024]{4,0,3,2,1:T(8,128)} %get-tuple-element.13), channel_id=1, source_target_pairs={{0,1},{1,2},{2,3},{3,4},{4,5},{5,6},{6,7},{7,8},{8,9},{9,10},{10,1... | collective-permute-start | bytes 2359304 | tf_op jit(solution)/shard_map/ppermute | solution.py:21
  136.5 1.5 fusion.103
  137.9 2.7 slice.272
  140.7 1.0 slice.273
  141.7 6.7 %fusion.102 = (f32[32,6,8,1,1023]{4,0,3,2,1:T(8,128)}, f32[32,6,8,1,1023]{4,0,3,2,1:T(8,128)}) fusion(f32[32,6,8,1,1024]{4,0,3,2,1:T(8,128)S(1)} %fusion.27), kind=kLoop, calls=%fused_computation.180 | loop fusion | bytes 25141248 | tf_op jit(solution)/shard_map/jit(_roll_static)/slice | solution.py:33
  148.4 9.7 %fusion.18 = f32[32,6,8,1,1024]{4,0,3,2,1:T(8,128)S(1)} fusion(f32[32,6,8,1,1024]{4,0,3,2,1:T(8,128)S(1)} %fusion.27, f32[32,6,1,1,1024]{4,0,3,2,1:T(8,128)} %collective-permute-done.5, f32[32,6,1,1,1024]{4,0,3,2,1:T(8,128)} %collective-permute-done.4, f32[32,1,8,1,1024]{4,0,3,2,1:T(8,128)} %slice.273, f32[32,5,8,1,1024]{4,0,3,2,1:T(8,128)} %slice.272, ...), kind=kLoop, calls=%fused_computation.22 | loop fusion | flops 31457280 | bytes 33030912 | tf_op jit(solution)/shard_map/add | solution.py:37
  158.1 1.3 fusion.101
  159.4 1.3 collective-permute-start.6
  160.7 5.0 %collective-permute-start.7 = (f32[32,6,1,1,1024]{4,0,3,2,1:T(8,128)}, f32[32,6,1,1,1024]{4,0,3,2,1:T(8,128)}, u32[]{:S(2)}, u32[]{:S(2)}) collective-permute-start(f32[32,6,1,1,1024]{4,0,3,2,1:T(8,128)} %get-tuple-element.7), channel_id=1, source_target_pairs={{0,1},{1,2},{2,3},{3,4},{4,5},{5,6},{6,7},{7,8},{8,9},{9,10},{10,1... | collective-permute-start | bytes 2359304 | tf_op jit(solution)/shard_map/ppermute | solution.py:21
  165.7 1.5 fusion.100
  167.2 11.2 %fusion.99 = (f32[32,6,8,1,1023]{4,0,3,2,1:T(8,128)}, f32[32,6,8,1,1023]{4,0,3,2,1:T(8,128)}) fusion(f32[32,6,8,1,1024]{4,0,3,2,1:T(8,128)} %copy-done.1), kind=kLoop, calls=%fused_computation.177 | loop fusion | bytes 25141248 | tf_op jit(solution)/shard_map/jit(_roll_static)/slice | solution.py:33
  178.4 13.5 %fusion.9 = bf16[32,6,8,1,1024]{4,0,3,2,1:T(8,128)(2,1)} fusion(f32[32,6,8,1,1024]{4,0,3,2,1:T(8,128)} %copy-done.1, f32[32,6,1,1,1024]{4,0,3,2,1:T(8,128)} %collective-permute-done.7, f32[32,6,1,1,1024]{4,0,3,2,1:T(8,128)} %collective-permute-done.6, f32[32,1,8,1,1024]{4,0,3,2,1:T(8,128)S(1)} %slice-done.1, f32[32,5,8,1,1024]{4,0,3,2,1:T(8,128)S(1)} %slice-done, ...), kind=kLoop, calls=%fused_computation.11 | loop fusion | flops 33030144 | bytes 29885184 | tf_op jit(solution)/shard_map/convert_element_type | solution.py:54
  191.9 14.4 %copy.289 = bf16[32,6,8,1,1024]{0,2,3,1,4:T(8,128)(2,1)} copy(bf16[32,6,8,1,1024]{4,0,3,2,1:T(8,128)(2,1)} %fusion.9) | data formatting | bytes 6291456 | tf_op jit(solution)/shard_map/convert_element_type | solution.py:54
  206.2 19.7 %reshape.582 = bf16[2,2,393216]{2,1,0:T(2,128)(2,1)} reshape(bf16[1024,6,1,8,32]{4,3,2,1,0:T(8,128)(2,1)} %bitcast.94) | data formatting | bytes 6291456
  225.9 4.5 all-to-all-start
  231.2 33.9 %all-to-all-done = bf16[2,2,393216]{2,1,0:T(2,128)(2,1)S(1)} async-done(((bf16[2,2,393216]{2,1,0:T(2,128)(2,1)}), bf16[2,2,393216]{2,1,0:T(2,128)(2,1)S(1)}, u32[]{:S(2)}, u32[]{:S(2)}) %all-to-all-start) | async-done | bytes 3145760 | tf_op jit(solution)/shard_map/all_to_all | solution.py:55
  265.1 11.1 %reshape.583 = bf16[1024,6,1,8,32]{4,3,2,1,0:T(8,128)(2,1)} reshape(bf16[2,2,393216]{2,1,0:T(2,128)(2,1)S(1)} %all-to-all-done) | data formatting | bytes 6291456
  276.2 14.0 %copy.290 = bf16[32,6,8,1,1024]{4,2,3,1,0:T(8,128)(2,1)S(1)} copy(bf16[32,6,8,1,1024]{0,2,3,1,4:T(8,128)(2,1)} %bitcast.95) | data formatting | bytes 6291456 | tf_op jit(solution)/shard_map/all_to_all | solution.py:55
  290.1 7.2 %reshape.563 = f32[32,6,8,1,2,512]{5,4,2,1,0,3:T(2,128)} reshape(bf16[32,6,8,1,1024]{4,2,3,1,0:T(8,128)(2,1)S(1)} %copy.290) | data formatting | bytes 9437184 | tf_op jit(solution)/shard_map/convert_element_type | solution.py:58
  297.4 6.6 %copy.296 = f32[2,32,6,8,1,512]{5,3,2,1,0,4:T(8,128)} copy(f32[2,32,6,8,1,512]{5,0,3,2,1,4:T(2,128)} %bitcast.98) | data formatting | bytes 12582912 | tf_op jit(solution)/shard_map/convert_element_type | solution.py:58
  304.0 9.7 %copy.297 = f32[64,6,8,1,512]{0,4,3,2,1:T(8,128)} copy(f32[64,6,8,1,512]{4,2,1,0,3:T(8,128)} %bitcast.93) | data formatting | bytes 12582912 | tf_op jit(solution)/shard_map/convert_element_type | solution.py:58
  313.7 16.1 %gather_fusion = f32[1024,64]{1,0:T(8,128)} fusion(f32[64,6,8,1,512]{0,4,3,2,1:T(8,128)} %copy.297, s32[1024]{0:T(1024)S(1)} %fusion.84), kind=kCustom, calls=%fused_computation | custom fusion | bytes 540672 | tf_op jit(solution)/shard_map/gather | solution.py:71
  329.8 1.2 copy.298
  332.4 0.9 pad_maximum_fusion.18
  333.2 4.5 collective-permute-start.8
  337.7 1.5 collective-permute-start.9
  339.2 1.3 convert_reduce_fusion
  340.5 3.5 copy.319
  344.0 2.9 reduce_sum.54
  347.5 3.6 bitcast_subtract_fusion
  351.2 1.2 maximum_maximum_fusion
  352.4 1.4 fusion.50
  354.6 0.7 fusion.96
  361.4 8.8 %fusion.37 = bf16[64,6,8,1,512]{4,0,1,2,3:T(8,128)(2,1)S(1)} fusion(f32[6,8,512]{2,0,1:T(8,128)S(1)} %copy.293, f32[64,6,8,512]{3,2,1,0:T(8,128)S(1)} %bitcast_subtract_fusion, f32[8,64,64]{2,1,0:T(8,128)S(1)} %fusion.117, f32[8,64]{1,0:T(8,128)S(1)} %broadcast_divide_fusion, f32[8]{0:T(128)S(1)} %get-tuple-element.30), kind=kOutput, calls=%fused_computation.59 | convolution fusion | flops 1211203584 | bytes 9668640 | tf_op jit(solution)/shard_map/jfrlc,rje->efrlc/dot_general | solution.py:99
  370.2 3.4 copy.305
  373.6 3.9 all-to-all-start.1
  377.6 36.6 %all-gather = f32[2,32,12]{1,2,0:T(8,128)S(1)} all-gather(f32[1,32,12]{1,2,0:T(8,128)S(1)} %bitcast.109), channel_id=1, replica_groups=mesh['member'=2,'slab'=16] {'member'}, dimensions={0}, use_global_device_ids=true | all-gather | bytes 4608 | tf_op jit(solution)/shard_map/all_gather | solution.py:102
  414.5 44.4 %psum.7 = f32[64,64]{1,0:T(8,128)S(1)} all-reduce(f32[64,64]{1,0:T(8,128)S(1)} %fusion.78), channel_id=1, replica_groups=mesh['member'=2,'slab'=16] {'member','slab'}, use_global_device_ids=true, to_apply=%region_6.7 | all-reduce | flops 4096 | bytes 32768 | tf_op jit(solution)/shard_map/psum | solution.py:108
  458.9 0.8 convolution_add_fusion
  459.7 2.2 copy.306
  (108 shorter events, 11.0 us)
Async XLA Ops:
  0.6 15.8 %copy-start.2 = (f32[32,6,8,1,1024]{4,3,2,1,0:T(1,128)S(1)}, f32[32,6,8,1,1024]{4,3,2,1,0:T(1,128)}, u32[]{:S(2)}) copy-start(f32[32,6,8,1,1024]{4,3,2,1,0:T(1,128)} %param.7) | copy-start | bytes 18874372
  7.2 2.7 copy-start.3
  11.1 58.4 %collective-permute-start = (f32[32,6,1,1,1024]{4,0,3,2,1:T(8,128)}, f32[32,6,1,1,1024]{4,0,3,2,1:T(8,128)}, u32[]{:S(2)}, u32[]{:S(2)}) collective-permute-start(f32[32,6,1,1,1024]{4,0,3,2,1:T(8,128)} %get-tuple-element.24), channel_id=1, source_target_pairs={{1,0},{2,1},{3,2},{4,3},{5,4},{6,5},{7,6},{8,7},{9,8},{10,9},{11,1... | collective-permute-start | bytes 2359304 | tf_op jit(solution)/shard_map/ppermute | solution.py:24
  12.4 57.1 %collective-permute-start.1 = (f32[32,6,1,1,1024]{4,0,3,2,1:T(8,128)}, f32[32,6,1,1,1024]{4,0,3,2,1:T(8,128)}, u32[]{:S(2)}, u32[]{:S(2)}) collective-permute-start(f32[32,6,1,1,1024]{4,0,3,2,1:T(8,128)} %get-tuple-element.25), channel_id=1, source_target_pairs={{0,1},{1,2},{2,3},{3,4},{4,5},{5,6},{6,7},{7,8},{8,9},{9,10},{10,1... | collective-permute-start | bytes 2359304 | tf_op jit(solution)/shard_map/ppermute | solution.py:21
  48.4 4.0 slice-start.4
  48.4 5.5 %slice-start.9 = ((s8[6291456]{0:T(1024)(128)(4,1)}), s8[4194304]{0:T(1024)(128)(4,1)S(1)}, s32[]{:S(2)}) async-start(s8[6291456]{0:T(1024)(128)(4,1)} %bitcast.101), calls=%async_computation.11 | async-start | bytes 8388608
  52.6 1.2 copy-start.8
  52.6 1.1 copy-start.12
  52.6 1.6 slice-start.10
  52.6 3.2 slice-start.7
  53.7 2.5 slice-start.8
  54.2 6.3 %slice-start.2 = ((s8[6291456]{0:T(1024)(128)(4,1)}), s8[4194304]{0:T(1024)(128)(4,1)S(1)}, s32[]{:S(2)}) async-start(s8[6291456]{0:T(1024)(128)(4,1)} %bitcast.91), calls=%async_computation.4 | async-start | bytes 8388608
  55.8 4.7 %slice-start.3 = ((s8[6291456]{0:T(1024)(128)(4,1)}), s8[2097152]{0:T(1024)(128)(4,1)S(1)}, s32[]{:S(2)}) async-start(s8[6291456]{0:T(1024)(128)(4,1)} %bitcast.91), calls=%async_computation.5 | async-start | bytes 4194304
  60.5 9.0 %slice-start.5 = ((s8[6291456]{0:T(1024)(128)(4,1)}), s8[2097152]{0:T(1024)(128)(4,1)S(1)}, s32[]{:S(2)}) async-start(s8[6291456]{0:T(1024)(128)(4,1)} %bitcast.96), calls=%async_computation.7 | async-start | bytes 4194304
  62.9 6.6 %slice-start.6 = ((s8[6291456]{0:T(1024)(128)(4,1)}), s8[4194304]{0:T(1024)(128)(4,1)S(1)}, s32[]{:S(2)}) async-start(s8[6291456]{0:T(1024)(128)(4,1)} %bitcast.96), calls=%async_computation.8 | async-start | bytes 8388608
  90.0 13.1 %copy-start = (f32[32,6,8,1,1024]{4,0,3,2,1:T(8,128)}, f32[32,6,8,1,1024]{4,0,3,2,1:T(8,128)S(1)}, u32[]{:S(2)}) copy-start(f32[32,6,8,1,1024]{4,0,3,2,1:T(8,128)S(1)} %fusion.36) | copy-start | bytes 18874372
  91.4 18.4 %collective-permute-start.2 = (f32[32,6,1,1,1024]{4,0,3,2,1:T(8,128)}, f32[32,6,1,1,1024]{4,0,3,2,1:T(8,128)}, u32[]{:S(2)}, u32[]{:S(2)}) collective-permute-start(f32[32,6,1,1,1024]{4,0,3,2,1:T(8,128)} %get-tuple-element.18), channel_id=1, source_target_pairs={{1,0},{2,1},{3,2},{4,3},{5,4},{6,5},{7,6},{8,7},{9,8},{10,9},{11,1... | collective-permute-start | bytes 2359304 | tf_op jit(solution)/shard_map/ppermute | solution.py:24
  92.7 17.2 %collective-permute-start.3 = (f32[32,6,1,1,1024]{4,0,3,2,1:T(8,128)}, f32[32,6,1,1,1024]{4,0,3,2,1:T(8,128)}, u32[]{:S(2)}, u32[]{:S(2)}) collective-permute-start(f32[32,6,1,1,1024]{4,0,3,2,1:T(8,128)} %get-tuple-element.19), channel_id=1, source_target_pairs={{0,1},{1,2},{2,3},{3,4},{4,5},{5,6},{6,7},{7,8},{8,9},{9,10},{10,1... | collective-permute-start | bytes 2359304 | tf_op jit(solution)/shard_map/ppermute | solution.py:21
  125.2 23.2 %collective-permute-start.4 = (f32[32,6,1,1,1024]{4,0,3,2,1:T(8,128)}, f32[32,6,1,1,1024]{4,0,3,2,1:T(8,128)}, u32[]{:S(2)}, u32[]{:S(2)}) collective-permute-start(f32[32,6,1,1,1024]{4,0,3,2,1:T(8,128)} %get-tuple-element.12), channel_id=1, source_target_pairs={{1,0},{2,1},{3,2},{4,3},{5,4},{6,5},{7,6},{8,7},{9,8},{10,9},{11,1... | collective-permute-start | bytes 2359304 | tf_op jit(solution)/shard_map/ppermute | solution.py:24
  126.5 21.9 %collective-permute-start.5 = (f32[32,6,1,1,1024]{4,0,3,2,1:T(8,128)}, f32[32,6,1,1,1024]{4,0,3,2,1:T(8,128)}, u32[]{:S(2)}, u32[]{:S(2)}) collective-permute-start(f32[32,6,1,1,1024]{4,0,3,2,1:T(8,128)} %get-tuple-element.13), channel_id=1, source_target_pairs={{0,1},{1,2},{2,3},{3,4},{4,5},{5,6},{6,7},{7,8},{8,9},{9,10},{10,1... | collective-permute-start | bytes 2359304 | tf_op jit(solution)/shard_map/ppermute | solution.py:21
  158.0 9.1 %copy-start.1 = (f32[32,6,8,1,1024]{4,0,3,2,1:T(8,128)}, f32[32,6,8,1,1024]{4,0,3,2,1:T(8,128)S(1)}, u32[]{:S(2)}) copy-start(f32[32,6,8,1,1024]{4,0,3,2,1:T(8,128)S(1)} %fusion.18) | copy-start | bytes 18874372
  159.4 19.0 %collective-permute-start.6 = (f32[32,6,1,1,1024]{4,0,3,2,1:T(8,128)}, f32[32,6,1,1,1024]{4,0,3,2,1:T(8,128)}, u32[]{:S(2)}, u32[]{:S(2)}) collective-permute-start(f32[32,6,1,1,1024]{4,0,3,2,1:T(8,128)} %get-tuple-element.6), channel_id=1, source_target_pairs={{1,0},{2,1},{3,2},{4,3},{5,4},{6,5},{7,6},{8,7},{9,8},{10,9},{11,1... | collective-permute-start | bytes 2359304 | tf_op jit(solution)/shard_map/ppermute | solution.py:24
  160.7 17.7 %collective-permute-start.7 = (f32[32,6,1,1,1024]{4,0,3,2,1:T(8,128)}, f32[32,6,1,1,1024]{4,0,3,2,1:T(8,128)}, u32[]{:S(2)}, u32[]{:S(2)}) collective-permute-start(f32[32,6,1,1,1024]{4,0,3,2,1:T(8,128)} %get-tuple-element.7), channel_id=1, source_target_pairs={{0,1},{1,2},{2,3},{3,4},{4,5},{5,6},{6,7},{7,8},{8,9},{9,10},{10,1... | collective-permute-start | bytes 2359304 | tf_op jit(solution)/shard_map/ppermute | solution.py:21
  167.2 11.2 %slice-start = ((f32[32,6,8,1,1024]{4,0,3,2,1:T(8,128)}), f32[32,5,8,1,1024]{4,0,3,2,1:T(8,128)S(1)}, s32[]{:S(2)}) async-start(f32[32,6,8,1,1024]{4,0,3,2,1:T(8,128)} %copy-done.1), calls=%async_computation.2 | async-start | bytes 10485760 | tf_op jit(solution)/shard_map/jit(_roll_static)/slice | solution.py:41
  167.2 11.2 %slice-start.1 = ((f32[32,6,8,1,1024]{4,0,3,2,1:T(8,128)}), f32[32,1,8,1,1024]{4,0,3,2,1:T(8,128)S(1)}, s32[]{:S(2)}) async-start(f32[32,6,8,1,1024]{4,0,3,2,1:T(8,128)} %copy-done.1), calls=%async_computation.3 | async-start | bytes 2097152 | tf_op jit(solution)/shard_map/jit(_roll_static)/slice | solution.py:41
  225.9 4.7 %copy-start.15 = (s32[8]{0:T(128)S(1)}, s32[8]{0:T(128)}, u32[]{:S(2)}) copy-start(s32[8]{0:T(128)} %param.13) | copy-start | bytes 100
  225.9 5.2 %copy-start.11 = (s32[8,1,128]{2,1,0:T(1,128)S(1)}, s32[8,1,128]{2,1,0:T(1,128)}, u32[]{:S(2)}) copy-start(s32[8,1,128]{2,1,0:T(1,128)} %param.10) | copy-start | bytes 12292
  225.9 39.2 %all-to-all-start = ((bf16[2,2,393216]{2,1,0:T(2,128)(2,1)}), bf16[2,2,393216]{2,1,0:T(2,128)(2,1)S(1)}, u32[]{:S(2)}, u32[]{:S(2)}) async-start(bf16[2,2,393216]{2,1,0:T(2,128)(2,1)} %reshape.582), calls=%async_computation | async-start | bytes 6291456 | tf_op jit(solution)/shard_map/all_to_all | solution.py:55
  304.0 27.1 %copy-start.9 = (f32[8,1,128]{2,1,0:T(1,128)S(1)}, f32[8,1,128]{2,1,0:T(1,128)}, u32[]{:S(2)}) copy-start(f32[8,1,128]{2,1,0:T(1,128)} %param.12) | copy-start | bytes 12292
  304.0 27.1 %copy-start.10 = (f32[8,1,128]{2,1,0:T(1,128)S(1)}, f32[8,1,128]{2,1,0:T(1,128)}, u32[]{:S(2)}) copy-start(f32[8,1,128]{2,1,0:T(1,128)} %param.11) | copy-start | bytes 12292
  331.7 0.7 copy-start.4
  332.4 0.9 copy-start.6
  333.2 17.9 %collective-permute-start.8 = (f32[8,65,64]{1,2,0:T(8,128)}, f32[8,65,64]{1,2,0:T(8,128)S(1)}, u32[]{:S(2)}, u32[]{:S(2)}) collective-permute-start(f32[8,65,64]{1,2,0:T(8,128)} %pad_maximum_fusion.18), channel_id=1, source_target_pairs={{0,1},{1,2},{2,3},{3,4},{4,5},{5,6},{6,7},{7,8},{8,9},{9,10},{10,1... | collective-permute-start | bytes 399368 | tf_op jit(solution)/shard_map/ppermute | solution.py:21
  337.7 13.4 %collective-permute-start.9 = (f32[8,65,64]{1,2,0:T(8,128)}, f32[8,65,64]{1,2,0:T(8,128)}, u32[]{:S(2)}, u32[]{:S(2)}) collective-permute-start(f32[8,65,64]{1,2,0:T(8,128)} %pad_maximum_fusion.18), channel_id=1, source_target_pairs={{1,0},{2,1},{3,2},{4,3},{5,4},{6,5},{7,6},{8,7},{9,8},{10,9},{11,1... | collective-permute-start | bytes 399368 | tf_op jit(solution)/shard_map/ppermute | solution.py:24
  347.4 3.8 copy-start.5
  347.4 3.8 copy-start.7
  347.5 4.9 %copy-start.13 = (f32[8]{0:T(128)S(1)}, f32[8]{0:T(128)}, u32[]{:S(2)}) copy-start(f32[8]{0:T(128)} %get-tuple-element.39) | copy-start | bytes 100
  347.5 4.9 %copy-start.14 = (f32[8]{0:T(128)S(1)}, f32[8]{0:T(128)}, u32[]{:S(2)}) copy-start(f32[8]{0:T(128)} %get-tuple-element.40) | copy-start | bytes 100
  373.6 86.1 %all-to-all-start.1 = ((bf16[64,6,8,1,512]{4,2,3,1,0:T(8,128)(2,1)}), bf16[64,6,8,1,512]{4,2,3,1,0:T(8,128)(2,1)S(1)}, u32[]{:S(2)}, u32[]{:S(2)}) async-start(bf16[64,6,8,1,512]{4,2,3,1,0:T(8,128)(2,1)} %copy.305), calls=%async_computation.1 | async-start | bytes 6291456 | tf_op jit(solution)/shard_map/all_to_all | solution.py:101
where the time goes:
time: 468 us; the launch traced here: 462 us
  local copies, waits for them, and re-layouts  207 us (44%)
  blocking collectives  80.9 us (17%)
  other arithmetic  77.7 us (17%)
  starting transfers between devices  43.8 us (9%)
  waiting for transfers between devices  33.9 us (7%)
  matrix products  17.6 us (4%)
    unnamed x57, local copies, waits for them, and re-layouts  54.7 us
    slice x8, local copies, waits for them, and re-layouts, advance(): right_col = jnp.roll(middle, -1, 4)  50.3 us
    psum x1, blocking collectives, body(): summed = lax.psum(weight_rows, ('member', 'slab')) / regions  44.4 us
    add x3, other arithmetic, advance(): middle + diffusion * laplace - advection * (right_col - left_col)  44.2 us
    all_gather x1, blocking collectives, body(): every_param = lax.all_gather(params, 'member', axis=0, tiled=True)  36.6 us
    all_to_all x1, waiting for transfers between devices, body(): lax.all_to_all(propagate_timestep, 'member', split_axis=4, concat_axis=0,...  33.9 us
    ppermute x5, starting transfers between devices, with_halo(): lax.ppermute(lax.slice_in_dim(block, block.shape[dim] - width, None, axis...  28.7 us
    convert_element_type x3, local copies, waits for them, and re-layouts, body(): xfull = latitude_band.astype(jnp.float32)  23.5 us
  transfers between devices with their start and end apart: 12, of which 1 were waited for; matrix products, arithmetic and copies ran while one was open for 22% of the time, Pallas kernels for 0%

commit v1 on v0

--- a/solution.py
+++ b/solution.py
@@ -105,7 +105,7 @@
     weight_rows = jnp.sum(weights, axis=0)
     regions = rows * lax.axis_size("slab") * lax.axis_size("member")
     start = lax.axis_index("member") * members_here
-    summed = lax.psum(weight_rows, ("member", "slab")) / regions
+    summed = lax.psum(lax.psum(weight_rows, "slab"), "member") / regions
     own_cols = lax.dynamic_slice_in_dim(summed, start, members_here, 1)
     param_analysis = pbar + jnp.einsum("jk,je->ek", ppert, own_cols, precision=highest)
     return (analysis, param_analysis)

time: 468 us -> 493 us (1.053)
  blocking collectives: 80.9 us -> 106 us
    psum x1 -> x2, blocking collectives: 44.4 us -> 69.2 us  [body(): summed = lax.psum(lax.psum(weight_rows, 'slab'), 'member') / regions]
  transfers between devices with their start and end apart: 12 -> 12, of which waited for: 1 -> 1; matrix products, arithmetic and copies ran while one was open for 22% -> 21% of each run, Pallas kernels for 0% -> 0%
where the time goes in v1:
time: 493 us; the launch traced here: 487 us
  local copies, waits for them, and re-layouts  207 us (42%)
  blocking collectives  106 us (22%)
  other arithmetic  78.1 us (16%)
  starting transfers between devices  43.8 us (9%)
  waiting for transfers between devices  33.9 us (7%)
  matrix products  17.6 us (4%)
    psum x2, blocking collectives, body(): summed = lax.psum(lax.psum(weight_rows, 'slab'), 'member') / regions  69.2 us
    unnamed x57, local copies, waits for them, and re-layouts  54.6 us
    slice x8, local copies, waits for them, and re-layouts, advance(): right_col = jnp.roll(middle, -1, 4)  50.3 us
    add x3, other arithmetic, advance(): middle + diffusion * laplace - advection * (right_col - left_col)  44.3 us
    all_gather x1, blocking collectives, body(): every_param = lax.all_gather(params, 'member', axis=0, tiled=True)  36.6 us
    all_to_all x1, waiting for transfers between devices, body(): lax.all_to_all(propagate_timestep, 'member', split_axis=4, concat_axis=0,...  33.8 us
    ppermute x5, starting transfers between devices, with_halo(): lax.ppermute(lax.slice_in_dim(block, block.shape[dim] - width, None, axis...  28.8 us
    convert_element_type x3, local copies, waits for them, and re-layouts, body(): xfull = latitude_band.astype(jnp.float32)  23.5 us
  transfers between devices with their start and end apart: 12, of which 1 were waited for; matrix products, arithmetic and copies ran while one was open for 21% of the time, Pallas kernels for 0%

profile of v1, /device:TPU:0, one launch (start us, length us, event | category | flops | bytes accessed | tf_op | source)
XLA Modules:
  0.0 487.3 jit_solution(10367513589962342437)
XLA Ops:
  0.6 6.5 %copy.281 = f32[32,6,8,1,1024]{4,0,3,2,1:T(8,128)S(1)} copy(f32[32,6,8,1,1024]{4,3,2,1,0:T(1,128)} %param.7) | data formatting | bytes 12582912 | tf_op args[0]
  7.2 2.6 copy-done.3
  9.8 1.2 fusion.110
  11.1 1.3 collective-permute-start
  12.4 4.0 collective-permute-start.1
  16.4 18.9 %fusion.108 = (f32[32,6,8,1,1023]{4,3,2,1,0:T(1,128)}, f32[32,6,8,1,1023]{4,3,2,1,0:T(1,128)}) fusion(f32[32,6,8,1,1024]{4,3,2,1,0:T(1,128)S(1)} %copy-done.2), kind=kLoop, calls=%fused_computation.186 | loop fusion | bytes 25141248 | tf_op jit(solution)/shard_map/jit(_roll_static)/slice | solution.py:33
  35.3 13.1 %slice.204 = f32[32,5,8,1,1024]{4,3,2,1,0:T(1,128)} slice(f32[32,6,8,1,1024]{4,3,2,1,0:T(1,128)} %param.7), slice={[0:32], [1:6], [0:8], [0:1], [0:1024]} | slice | bytes 10485760 | tf_op jit(solution)/shard_map/jit(_roll_static)/slice | solution.py:41
  48.5 3.9 copy.324
  52.7 1.1 pad_maximum_fusion.10
  54.3 1.6 copy.320
  56.4 4.2 copy.323
  60.6 2.4 fusion.109
  63.0 6.6 %pad_maximum_fusion.8 = (f32[32,6,8,1,1024]{4,2,3,1,0:T(8,128)S(1)}, f32[32,6,8,1,1024]{4,2,3,1,0:T(8,128)}) fusion(f32[32,6,8,1,1]{4,2,3,1,0:T(8,128)S(1)} %bitcast.105, f32[32,6,8,1,1023]{4,2,3,1,0:T(8,128)S(1)} %copy.320, f32[32,6,8,1,1023]{4,2,3,1,0:T(8,128)} %copy.323, f32[32,6,8,1,1]{4,2,3,1,0:T(8,128)S(1)} %bitcast.106), kind=kLoop, calls=%fused_computation.46 | loop fusion | flops 3145728 | bytes 25165824 | tf_op jit(solution)/shard_map/jit(_roll_static)/concatenate | solution.py:33
  69.6 20.5 %fusion.36 = f32[32,6,8,1,1024]{4,0,3,2,1:T(8,128)S(1)} fusion(f32[32,6,8,1,1024]{4,0,3,2,1:T(8,128)S(1)} %bitcast.97, f32[32,6,1,1,1024]{4,0,3,2,1:T(8,128)} %collective-permute-done.1, f32[32,6,1,1,1024]{4,0,3,2,1:T(8,128)} %collective-permute-done, f32[32,6,8,1,1024]{4,2,3,1,0:T(8,128)S(1)} %pad_maximum_fusion.10, ...), kind=kLoop, calls=%fused_computation.44 | loop fusion | flops 26738688 | bytes 33030912 | tf_op jit(solution)/shard_map/add | solution.py:37
  90.1 1.4 fusion.107
  91.5 1.3 collective-permute-start.2
  92.8 5.2 %collective-permute-start.3 = (f32[32,6,1,1,1024]{4,0,3,2,1:T(8,128)}, f32[32,6,1,1,1024]{4,0,3,2,1:T(8,128)}, u32[]{:S(2)}, u32[]{:S(2)}) collective-permute-start(f32[32,6,1,1,1024]{4,0,3,2,1:T(8,128)} %get-tuple-element.19), channel_id=1, source_target_pairs={{0,1},{1,2},{2,3},{3,4},{4,5},{5,6},{6,7},{7,8},{8,9},{9,10},{10,1... | collective-permute-start | bytes 2359304 | tf_op jit(solution)/shard_map/ppermute | solution.py:21
  98.0 1.4 fusion.106
  99.5 2.7 slice.264
  102.2 1.0 slice.265
  103.2 6.7 %fusion.105 = (f32[32,6,8,1,1023]{4,0,3,2,1:T(8,128)}, f32[32,6,8,1,1023]{4,0,3,2,1:T(8,128)}) fusion(f32[32,6,8,1,1024]{4,0,3,2,1:T(8,128)S(1)} %fusion.36), kind=kLoop, calls=%fused_computation.183 | loop fusion | bytes 25141248 | tf_op jit(solution)/shard_map/jit(_roll_static)/slice | solution.py:33
  109.9 14.1 %fusion.27 = f32[32,6,8,1,1024]{4,0,3,2,1:T(8,128)S(1)} fusion(f32[32,6,8,1,1024]{4,0,3,2,1:T(8,128)} %copy-done, f32[32,6,1,1,1024]{4,0,3,2,1:T(8,128)} %collective-permute-done.3, f32[32,6,1,1,1024]{4,0,3,2,1:T(8,128)} %collective-permute-done.2, f32[32,1,8,1,1024]{4,0,3,2,1:T(8,128)} %slice.265, f32[32,5,8,1,1024]{4,0,3,2,1:T(8,128)} %slice.264, ...), kind=kLoop, calls=%fused_computation.33 | loop fusion | flops 31457280 | bytes 33030912 | tf_op jit(solution)/shard_map/add | solution.py:37
  124.1 1.3 fusion.104
  125.4 1.3 collective-permute-start.4
  126.6 10.0 %collective-permute-start.5 = (f32[32,6,1,1,1024]{4,0,3,2,1:T(8,128)}, f32[32,6,1,1,1024]{4,0,3,2,1:T(8,128)}, u32[]{:S(2)}, u32[]{:S(2)}) collective-permute-start(f32[32,6,1,1,1024]{4,0,3,2,1:T(8,128)} %get-tuple-element.13), channel_id=1, source_target_pairs={{0,1},{1,2},{2,3},{3,4},{4,5},{5,6},{6,7},{7,8},{8,9},{9,10},{10,1... | collective-permute-start | bytes 2359304 | tf_op jit(solution)/shard_map/ppermute | solution.py:21
  136.6 1.5 fusion.103
  138.1 2.7 slice.272
  140.8 1.0 slice.273
  141.8 6.7 %fusion.102 = (f32[32,6,8,1,1023]{4,0,3,2,1:T(8,128)}, f32[32,6,8,1,1023]{4,0,3,2,1:T(8,128)}) fusion(f32[32,6,8,1,1024]{4,0,3,2,1:T(8,128)S(1)} %fusion.27), kind=kLoop, calls=%fused_computation.180 | loop fusion | bytes 25141248 | tf_op jit(solution)/shard_map/jit(_roll_static)/slice | solution.py:33
  148.5 9.7 %fusion.18 = f32[32,6,8,1,1024]{4,0,3,2,1:T(8,128)S(1)} fusion(f32[32,6,8,1,1024]{4,0,3,2,1:T(8,128)S(1)} %fusion.27, f32[32,6,1,1,1024]{4,0,3,2,1:T(8,128)} %collective-permute-done.5, f32[32,6,1,1,1024]{4,0,3,2,1:T(8,128)} %collective-permute-done.4, f32[32,1,8,1,1024]{4,0,3,2,1:T(8,128)} %slice.273, f32[32,5,8,1,1024]{4,0,3,2,1:T(8,128)} %slice.272, ...), kind=kLoop, calls=%fused_computation.22 | loop fusion | flops 31457280 | bytes 33030912 | tf_op jit(solution)/shard_map/add | solution.py:37
  158.2 1.3 fusion.101
  159.5 1.3 collective-permute-start.6
  160.8 5.0 %collective-permute-start.7 = (f32[32,6,1,1,1024]{4,0,3,2,1:T(8,128)}, f32[32,6,1,1,1024]{4,0,3,2,1:T(8,128)}, u32[]{:S(2)}, u32[]{:S(2)}) collective-permute-start(f32[32,6,1,1,1024]{4,0,3,2,1:T(8,128)} %get-tuple-element.7), channel_id=1, source_target_pairs={{0,1},{1,2},{2,3},{3,4},{4,5},{5,6},{6,7},{7,8},{8,9},{9,10},{10,1... | collective-permute-start | bytes 2359304 | tf_op jit(solution)/shard_map/ppermute | solution.py:21
  165.9 1.5 fusion.100
  167.3 11.2 %fusion.99 = (f32[32,6,8,1,1023]{4,0,3,2,1:T(8,128)}, f32[32,6,8,1,1023]{4,0,3,2,1:T(8,128)}) fusion(f32[32,6,8,1,1024]{4,0,3,2,1:T(8,128)} %copy-done.1), kind=kLoop, calls=%fused_computation.177 | loop fusion | bytes 25141248 | tf_op jit(solution)/shard_map/jit(_roll_static)/slice | solution.py:33
  178.5 13.7 %fusion.9 = bf16[32,6,8,1,1024]{4,0,3,2,1:T(8,128)(2,1)} fusion(f32[32,6,8,1,1024]{4,0,3,2,1:T(8,128)} %copy-done.1, f32[32,6,1,1,1024]{4,0,3,2,1:T(8,128)} %collective-permute-done.7, f32[32,6,1,1,1024]{4,0,3,2,1:T(8,128)} %collective-permute-done.6, f32[32,1,8,1,1024]{4,0,3,2,1:T(8,128)S(1)} %slice-done.1, f32[32,5,8,1,1024]{4,0,3,2,1:T(8,128)S(1)} %slice-done, ...), kind=kLoop, calls=%fused_computation.11 | loop fusion | flops 33030144 | bytes 29885184 | tf_op jit(solution)/shard_map/convert_element_type | solution.py:54
  192.3 14.4 %copy.289 = bf16[32,6,8,1,1024]{0,2,3,1,4:T(8,128)(2,1)} copy(bf16[32,6,8,1,1024]{4,0,3,2,1:T(8,128)(2,1)} %fusion.9) | data formatting | bytes 6291456 | tf_op jit(solution)/shard_map/convert_element_type | solution.py:54
  206.7 19.7 %reshape.582 = bf16[2,2,393216]{2,1,0:T(2,128)(2,1)} reshape(bf16[1024,6,1,8,32]{4,3,2,1,0:T(8,128)(2,1)} %bitcast.94) | data formatting | bytes 6291456
  226.4 4.5 all-to-all-start
  231.7 33.8 %all-to-all-done = bf16[2,2,393216]{2,1,0:T(2,128)(2,1)S(1)} async-done(((bf16[2,2,393216]{2,1,0:T(2,128)(2,1)}), bf16[2,2,393216]{2,1,0:T(2,128)(2,1)S(1)}, u32[]{:S(2)}, u32[]{:S(2)}) %all-to-all-start) | async-done | bytes 3145760 | tf_op jit(solution)/shard_map/all_to_all | solution.py:55
  265.5 11.0 %reshape.583 = bf16[1024,6,1,8,32]{4,3,2,1,0:T(8,128)(2,1)} reshape(bf16[2,2,393216]{2,1,0:T(2,128)(2,1)S(1)} %all-to-all-done) | data formatting | bytes 6291456
  276.6 14.0 %copy.290 = bf16[32,6,8,1,1024]{4,2,3,1,0:T(8,128)(2,1)S(1)} copy(bf16[32,6,8,1,1024]{0,2,3,1,4:T(8,128)(2,1)} %bitcast.95) | data formatting | bytes 6291456 | tf_op jit(solution)/shard_map/all_to_all | solution.py:55
  290.5 7.2 %reshape.563 = f32[32,6,8,1,2,512]{5,4,2,1,0,3:T(2,128)} reshape(bf16[32,6,8,1,1024]{4,2,3,1,0:T(8,128)(2,1)S(1)} %copy.290) | data formatting | bytes 9437184 | tf_op jit(solution)/shard_map/convert_element_type | solution.py:58
  297.8 6.6 %copy.296 = f32[2,32,6,8,1,512]{5,3,2,1,0,4:T(8,128)} copy(f32[2,32,6,8,1,512]{5,0,3,2,1,4:T(2,128)} %bitcast.98) | data formatting | bytes 12582912 | tf_op jit(solution)/shard_map/convert_element_type | solution.py:58
  304.4 9.7 %copy.297 = f32[64,6,8,1,512]{0,4,3,2,1:T(8,128)} copy(f32[64,6,8,1,512]{4,2,1,0,3:T(8,128)} %bitcast.93) | data formatting | bytes 12582912 | tf_op jit(solution)/shard_map/convert_element_type | solution.py:58
  314.1 16.2 %gather_fusion = f32[1024,64]{1,0:T(8,128)} fusion(f32[64,6,8,1,512]{0,4,3,2,1:T(8,128)} %copy.297, s32[1024]{0:T(1024)S(1)} %fusion.84), kind=kCustom, calls=%fused_computation | custom fusion | bytes 540672 | tf_op jit(solution)/shard_map/gather | solution.py:71
  330.3 1.2 copy.298
  332.8 0.9 pad_maximum_fusion.18
  333.7 4.5 collective-permute-start.8
  338.2 1.5 collective-permute-start.9
  339.6 1.3 convert_reduce_fusion
  341.0 3.5 copy.319
  344.5 2.9 reduce_sum.54
  347.9 3.6 bitcast_subtract_fusion
  351.7 1.2 maximum_maximum_fusion
  352.9 1.4 fusion.50
  361.9 8.8 %fusion.37 = bf16[64,6,8,1,512]{4,0,1,2,3:T(8,128)(2,1)S(1)} fusion(f32[6,8,512]{2,0,1:T(8,128)S(1)} %copy.293, f32[64,6,8,512]{3,2,1,0:T(8,128)S(1)} %bitcast_subtract_fusion, f32[8,64,64]{2,1,0:T(8,128)S(1)} %fusion.117, f32[8,64]{1,0:T(8,128)S(1)} %broadcast_divide_fusion, f32[8]{0:T(128)S(1)} %get-tuple-element.30), kind=kOutput, calls=%fused_computation.59 | convolution fusion | flops 1211203584 | bytes 9668640 | tf_op jit(solution)/shard_map/jfrlc,rje->efrlc/dot_general | solution.py:99
  370.6 3.4 copy.305
  374.1 3.9 all-to-all-start.1
  378.0 36.6 %all-gather = f32[2,32,12]{1,2,0:T(8,128)S(1)} all-gather(f32[1,32,12]{1,2,0:T(8,128)S(1)} %bitcast.109), channel_id=1, replica_groups=mesh['member'=2,'slab'=16] {'member'}, dimensions={0}, use_global_device_ids=true | all-gather | bytes 4608 | tf_op jit(solution)/shard_map/all_gather | solution.py:102
  414.9 61.8 %psum.14 = f32[64,64]{1,0:T(8,128)S(1)} all-reduce(f32[64,64]{1,0:T(8,128)S(1)} %fusion.78), channel_id=1, replica_groups=mesh['member'=2,'slab'=16] {'slab'}, use_global_device_ids=true, to_apply=%region_6.7 | all-reduce | flops 4096 | bytes 32768 | tf_op jit(solution)/shard_map/psum | solution.py:108
  476.7 7.4 %psum.15 = f32[64,64]{1,0:T(8,128)S(1)} all-reduce(f32[64,64]{1,0:T(8,128)S(1)} %psum.14), channel_id=1, replica_groups=mesh['member'=2,'slab'=16] {'member'}, use_global_device_ids=true, to_apply=%region_7.8 | all-reduce | flops 4096 | bytes 32768 | tf_op jit(solution)/shard_map/psum | solution.py:108
  484.1 0.8 convolution_add_fusion
  484.9 2.2 copy.306
  (109 shorter events, 11.7 us)
Async XLA Ops:
  0.6 15.8 %copy-start.2 = (f32[32,6,8,1,1024]{4,3,2,1,0:T(1,128)S(1)}, f32[32,6,8,1,1024]{4,3,2,1,0:T(1,128)}, u32[]{:S(2)}) copy-start(f32[32,6,8,1,1024]{4,3,2,1,0:T(1,128)} %param.7) | copy-start | bytes 18874372
  7.2 2.7 copy-start.3
  11.1 58.5 %collective-permute-start = (f32[32,6,1,1,1024]{4,0,3,2,1:T(8,128)}, f32[32,6,1,1,1024]{4,0,3,2,1:T(8,128)}, u32[]{:S(2)}, u32[]{:S(2)}) collective-permute-start(f32[32,6,1,1,1024]{4,0,3,2,1:T(8,128)} %get-tuple-element.24), channel_id=1, source_target_pairs={{1,0},{2,1},{3,2},{4,3},{5,4},{6,5},{7,6},{8,7},{9,8},{10,9},{11,1... | collective-permute-start | bytes 2359304 | tf_op jit(solution)/shard_map/ppermute | solution.py:24
  12.4 57.2 %collective-permute-start.1 = (f32[32,6,1,1,1024]{4,0,3,2,1:T(8,128)}, f32[32,6,1,1,1024]{4,0,3,2,1:T(8,128)}, u32[]{:S(2)}, u32[]{:S(2)}) collective-permute-start(f32[32,6,1,1,1024]{4,0,3,2,1:T(8,128)} %get-tuple-element.25), channel_id=1, source_target_pairs={{0,1},{1,2},{2,3},{3,4},{4,5},{5,6},{6,7},{7,8},{8,9},{9,10},{10,1... | collective-permute-start | bytes 2359304 | tf_op jit(solution)/shard_map/ppermute | solution.py:21
  48.5 4.0 slice-start.4
  48.5 5.5 %slice-start.9 = ((s8[6291456]{0:T(1024)(128)(4,1)}), s8[4194304]{0:T(1024)(128)(4,1)S(1)}, s32[]{:S(2)}) async-start(s8[6291456]{0:T(1024)(128)(4,1)} %bitcast.101), calls=%async_computation.11 | async-start | bytes 8388608
  52.6 1.2 copy-start.8
  52.7 1.1 copy-start.12
  52.7 1.6 slice-start.10
  52.7 3.2 slice-start.7
  53.8 2.5 slice-start.8
  54.3 6.3 %slice-start.2 = ((s8[6291456]{0:T(1024)(128)(4,1)}), s8[4194304]{0:T(1024)(128)(4,1)S(1)}, s32[]{:S(2)}) async-start(s8[6291456]{0:T(1024)(128)(4,1)} %bitcast.91), calls=%async_computation.4 | async-start | bytes 8388608
  55.9 4.7 slice-start.3
  60.6 9.0 %slice-start.5 = ((s8[6291456]{0:T(1024)(128)(4,1)}), s8[2097152]{0:T(1024)(128)(4,1)S(1)}, s32[]{:S(2)}) async-start(s8[6291456]{0:T(1024)(128)(4,1)} %bitcast.96), calls=%async_computation.7 | async-start | bytes 4194304
  63.0 6.6 %slice-start.6 = ((s8[6291456]{0:T(1024)(128)(4,1)}), s8[4194304]{0:T(1024)(128)(4,1)S(1)}, s32[]{:S(2)}) async-start(s8[6291456]{0:T(1024)(128)(4,1)} %bitcast.96), calls=%async_computation.8 | async-start | bytes 8388608
  90.1 13.1 %copy-start = (f32[32,6,8,1,1024]{4,0,3,2,1:T(8,128)}, f32[32,6,8,1,1024]{4,0,3,2,1:T(8,128)S(1)}, u32[]{:S(2)}) copy-start(f32[32,6,8,1,1024]{4,0,3,2,1:T(8,128)S(1)} %fusion.36) | copy-start | bytes 18874372
  91.5 18.4 %collective-permute-start.2 = (f32[32,6,1,1,1024]{4,0,3,2,1:T(8,128)}, f32[32,6,1,1,1024]{4,0,3,2,1:T(8,128)}, u32[]{:S(2)}, u32[]{:S(2)}) collective-permute-start(f32[32,6,1,1,1024]{4,0,3,2,1:T(8,128)} %get-tuple-element.18), channel_id=1, source_target_pairs={{1,0},{2,1},{3,2},{4,3},{5,4},{6,5},{7,6},{8,7},{9,8},{10,9},{11,1... | collective-permute-start | bytes 2359304 | tf_op jit(solution)/shard_map/ppermute | solution.py:24
  92.8 17.1 %collective-permute-start.3 = (f32[32,6,1,1,1024]{4,0,3,2,1:T(8,128)}, f32[32,6,1,1,1024]{4,0,3,2,1:T(8,128)}, u32[]{:S(2)}, u32[]{:S(2)}) collective-permute-start(f32[32,6,1,1,1024]{4,0,3,2,1:T(8,128)} %get-tuple-element.19), channel_id=1, source_target_pairs={{0,1},{1,2},{2,3},{3,4},{4,5},{5,6},{6,7},{7,8},{8,9},{9,10},{10,1... | collective-permute-start | bytes 2359304 | tf_op jit(solution)/shard_map/ppermute | solution.py:21
  125.4 23.2 %collective-permute-start.4 = (f32[32,6,1,1,1024]{4,0,3,2,1:T(8,128)}, f32[32,6,1,1,1024]{4,0,3,2,1:T(8,128)}, u32[]{:S(2)}, u32[]{:S(2)}) collective-permute-start(f32[32,6,1,1,1024]{4,0,3,2,1:T(8,128)} %get-tuple-element.12), channel_id=1, source_target_pairs={{1,0},{2,1},{3,2},{4,3},{5,4},{6,5},{7,6},{8,7},{9,8},{10,9},{11,1... | collective-permute-start | bytes 2359304 | tf_op jit(solution)/shard_map/ppermute | solution.py:24
  126.6 21.9 %collective-permute-start.5 = (f32[32,6,1,1,1024]{4,0,3,2,1:T(8,128)}, f32[32,6,1,1,1024]{4,0,3,2,1:T(8,128)}, u32[]{:S(2)}, u32[]{:S(2)}) collective-permute-start(f32[32,6,1,1,1024]{4,0,3,2,1:T(8,128)} %get-tuple-element.13), channel_id=1, source_target_pairs={{0,1},{1,2},{2,3},{3,4},{4,5},{5,6},{6,7},{7,8},{8,9},{9,10},{10,1... | collective-permute-start | bytes 2359304 | tf_op jit(solution)/shard_map/ppermute | solution.py:21
  158.2 9.2 %copy-start.1 = (f32[32,6,8,1,1024]{4,0,3,2,1:T(8,128)}, f32[32,6,8,1,1024]{4,0,3,2,1:T(8,128)S(1)}, u32[]{:S(2)}) copy-start(f32[32,6,8,1,1024]{4,0,3,2,1:T(8,128)S(1)} %fusion.18) | copy-start | bytes 18874372
  159.5 19.0 %collective-permute-start.6 = (f32[32,6,1,1,1024]{4,0,3,2,1:T(8,128)}, f32[32,6,1,1,1024]{4,0,3,2,1:T(8,128)}, u32[]{:S(2)}, u32[]{:S(2)}) collective-permute-start(f32[32,6,1,1,1024]{4,0,3,2,1:T(8,128)} %get-tuple-element.6), channel_id=1, source_target_pairs={{1,0},{2,1},{3,2},{4,3},{5,4},{6,5},{7,6},{8,7},{9,8},{10,9},{11,1... | collective-permute-start | bytes 2359304 | tf_op jit(solution)/shard_map/ppermute | solution.py:24
  160.8 17.7 %collective-permute-start.7 = (f32[32,6,1,1,1024]{4,0,3,2,1:T(8,128)}, f32[32,6,1,1,1024]{4,0,3,2,1:T(8,128)}, u32[]{:S(2)}, u32[]{:S(2)}) collective-permute-start(f32[32,6,1,1,1024]{4,0,3,2,1:T(8,128)} %get-tuple-element.7), channel_id=1, source_target_pairs={{0,1},{1,2},{2,3},{3,4},{4,5},{5,6},{6,7},{7,8},{8,9},{9,10},{10,1... | collective-permute-start | bytes 2359304 | tf_op jit(solution)/shard_map/ppermute | solution.py:21
  167.3 11.2 %slice-start = ((f32[32,6,8,1,1024]{4,0,3,2,1:T(8,128)}), f32[32,5,8,1,1024]{4,0,3,2,1:T(8,128)S(1)}, s32[]{:S(2)}) async-start(f32[32,6,8,1,1024]{4,0,3,2,1:T(8,128)} %copy-done.1), calls=%async_computation.2 | async-start | bytes 10485760 | tf_op jit(solution)/shard_map/jit(_roll_static)/slice | solution.py:41
  167.3 11.2 %slice-start.1 = ((f32[32,6,8,1,1024]{4,0,3,2,1:T(8,128)}), f32[32,1,8,1,1024]{4,0,3,2,1:T(8,128)S(1)}, s32[]{:S(2)}) async-start(f32[32,6,8,1,1024]{4,0,3,2,1:T(8,128)} %copy-done.1), calls=%async_computation.3 | async-start | bytes 2097152 | tf_op jit(solution)/shard_map/jit(_roll_static)/slice | solution.py:41
  226.4 4.7 copy-start.15
  226.4 5.3 %copy-start.11 = (s32[8,1,128]{2,1,0:T(1,128)S(1)}, s32[8,1,128]{2,1,0:T(1,128)}, u32[]{:S(2)}) copy-start(s32[8,1,128]{2,1,0:T(1,128)} %param.10) | copy-start | bytes 12292
  226.4 39.2 %all-to-all-start = ((bf16[2,2,393216]{2,1,0:T(2,128)(2,1)}), bf16[2,2,393216]{2,1,0:T(2,128)(2,1)S(1)}, u32[]{:S(2)}, u32[]{:S(2)}) async-start(bf16[2,2,393216]{2,1,0:T(2,128)(2,1)} %reshape.582), calls=%async_computation | async-start | bytes 6291456 | tf_op jit(solution)/shard_map/all_to_all | solution.py:55
  304.4 27.1 %copy-start.9 = (f32[8,1,128]{2,1,0:T(1,128)S(1)}, f32[8,1,128]{2,1,0:T(1,128)}, u32[]{:S(2)}) copy-start(f32[8,1,128]{2,1,0:T(1,128)} %param.12) | copy-start | bytes 12292
  304.4 27.1 %copy-start.10 = (f32[8,1,128]{2,1,0:T(1,128)S(1)}, f32[8,1,128]{2,1,0:T(1,128)}, u32[]{:S(2)}) copy-start(f32[8,1,128]{2,1,0:T(1,128)} %param.11) | copy-start | bytes 12292
  332.1 0.7 copy-start.4
  332.8 0.9 copy-start.6
  333.7 17.9 %collective-permute-start.8 = (f32[8,65,64]{1,2,0:T(8,128)}, f32[8,65,64]{1,2,0:T(8,128)S(1)}, u32[]{:S(2)}, u32[]{:S(2)}) collective-permute-start(f32[8,65,64]{1,2,0:T(8,128)} %pad_maximum_fusion.18), channel_id=1, source_target_pairs={{0,1},{1,2},{2,3},{3,4},{4,5},{5,6},{6,7},{7,8},{8,9},{9,10},{10,1... | collective-permute-start | bytes 399368 | tf_op jit(solution)/shard_map/ppermute | solution.py:21
  338.2 13.5 %collective-permute-start.9 = (f32[8,65,64]{1,2,0:T(8,128)}, f32[8,65,64]{1,2,0:T(8,128)}, u32[]{:S(2)}, u32[]{:S(2)}) collective-permute-start(f32[8,65,64]{1,2,0:T(8,128)} %pad_maximum_fusion.18), channel_id=1, source_target_pairs={{1,0},{2,1},{3,2},{4,3},{5,4},{6,5},{7,6},{8,7},{9,8},{10,9},{11,1... | collective-permute-start | bytes 399368 | tf_op jit(solution)/shard_map/ppermute | solution.py:24
  347.9 3.8 copy-start.5
  347.9 3.8 copy-start.7
  347.9 4.9 %copy-start.13 = (f32[8]{0:T(128)S(1)}, f32[8]{0:T(128)}, u32[]{:S(2)}) copy-start(f32[8]{0:T(128)} %get-tuple-element.39) | copy-start | bytes 100
  347.9 4.9 %copy-start.14 = (f32[8]{0:T(128)S(1)}, f32[8]{0:T(128)}, u32[]{:S(2)}) copy-start(f32[8]{0:T(128)} %get-tuple-element.40) | copy-start | bytes 100
  374.1 110.9 %all-to-all-start.1 = ((bf16[64,6,8,1,512]{4,2,3,1,0:T(8,128)(2,1)}), bf16[64,6,8,1,512]{4,2,3,1,0:T(8,128)(2,1)S(1)}, u32[]{:S(2)}, u32[]{:S(2)}) async-start(bf16[64,6,8,1,512]{4,2,3,1,0:T(8,128)(2,1)} %copy.305), calls=%async_computation.1 | async-start | bytes 6291456 | tf_op jit(solution)/shard_map/all_to_all | solution.py:101
